TPU v7x, 256 devices: a whole 4x4x8 slice. The times are simulated.
256 devices in a mesh: section: 4 (over x_lo, core), row: 8 (over z), col: 8 (over x_hi, y).
Axes of the slice: x: 4 (x_hi: 2, x_lo: 2; x = x_hi * 2 + x_lo), y: 4, z: 8, core: 2. Of those that a mesh axis runs over, the one named last changes fastest.
Arguments:
- images: bfloat16 [4, 8, 80, 80, 512], P('section', None, 'row', 'col'), may hold values from -6 to 6
- block_in: bfloat16 [512, 256], replicated, may hold values from -0.25 to 0.25
- block_grouped_one: bfloat16 [1152, 256], replicated, may hold values from -0.1875 to 0.1875
- block_grouped_two: bfloat16 [1152, 256], replicated, may hold values from -0.1875 to 0.1875
- block_out: bfloat16 [256, 512], replicated, may hold values from -0.375 to 0.375
- trans_in: bfloat16 [512, 768], replicated, may hold values from -0.25 to 0.25
- trans_grouped_one: bfloat16 [1152, 768], replicated, may hold values from -0.1875 to 0.1875
- trans_grouped_two: bfloat16 [1152, 768], replicated, may hold values from -0.1875 to 0.1875
- trans_out: bfloat16 [768, 1536], replicated, may hold values from -0.21875 to 0.21875
- trans_short: bfloat16 [512, 1536], replicated, may hold values from -0.25 to 0.25
Outputs:
- features: bfloat16 [4, 8, 40, 40, 1536], P('section', 'row', 'col')
All inputs are finite; a program needn't handle non-finite values.
Results may differ from a plain program's by a relative error of at most 0.012.
Values may be sent and summed in bfloat16 or wider, within the bound.
A program may use at most 64 MiB of HBM per device.

v0:
```python
import jax
import jax.numpy as jnp
from jax import lax
from jax.sharding import PartitionSpec as P

GELU_GAIN = 1.7015
RESIDUAL_SCALE = 0.2
BETA_BLOCK = 0.9805
BETA_TRANSITION = 0.9623


def with_halo(block, sides, width):
    for axis, dim in sides:
        count = lax.axis_size(axis)
        forward = [(i, i + 1) for i in range(count - 1)]
        backward = [(target, source) for source, target in forward]
        low = lax.ppermute(
            lax.slice_in_dim(block, block.shape[dim] - width, None, axis=dim), axis, forward
        )
        high = lax.ppermute(lax.slice_in_dim(block, 0, width, axis=dim), axis, backward)
        block = jnp.concatenate([low, block, high], axis=dim)
    return block


def activate(values):
    return GELU_GAIN * jax.nn.gelu(values, approximate=True)


def matmul_rows(tensor, weight):
    shaped = tensor.shape
    result = jnp.dot(tensor.reshape(-1, shaped[-1]), weight, preferred_element_type=jnp.float32)
    return result.reshape(shaped[:-1] + (weight.shape[1],))


def group_conv(padded, weight, stride):
    lot_count, image_count, height, breadth, channels = padded.shape
    batches = lot_count * image_count
    merged = padded.reshape(batches, height, breadth, channels)
    group_width = weight.shape[0] // 9
    out_height = (height - 2) // stride
    out_breadth = (breadth - 2) // stride
    offset = stride - 1
    tap_list = []
    for row_tap in range(3):
        for col_tap in range(3):
            start_row = offset + row_tap
            start_col = offset + col_tap
            tap_list.append(
                lax.slice(
                    merged,
                    (0, start_row, start_col, 0),
                    (
                        batches,
                        start_row + stride * (out_height - 1) + 1,
                        start_col + stride * (out_breadth - 1) + 1,
                        channels,
                    ),
                    (1, stride, stride, 1),
                )
            )
    stacked = jnp.stack(tap_list, axis=3)
    groups = channels // group_width
    stacked = stacked.reshape(batches, out_height, out_breadth, 9, groups, group_width)
    kernel = weight.reshape(9, group_width, groups, group_width)
    result = jnp.einsum("nhwtgc,tcgd->nhwgd", stacked, kernel, preferred_element_type=jnp.float32)
    return result.reshape(lot_count, image_count, out_height, out_breadth, channels)


def plane_rims(tensor):
    return with_halo(tensor, (("row", 2), ("col", 3)), 1)


def strip_rims(tensor):
    padded = with_halo(tensor, (("col", 2),), 1)
    return jnp.pad(padded, ((0, 0), (0, 0), (0, 0), (1, 1), (0, 0)))


def relayout(tensor):
    return lax.all_to_all(
        lax.all_to_all(tensor, "row", split_axis=1, concat_axis=2, tiled=True),
        "col",
        split_axis=2,
        concat_axis=3,
        tiled=True,
    )


def transition(block_result, weights_all, rims):
    trans_in, trans_grouped_one, trans_grouped_two, trans_out, trans_short = weights_all
    lot_count, image_count, height, breadth, channels = block_result.shape
    pre_trans = (activate(block_result.astype(jnp.float32)) * BETA_TRANSITION).astype(jnp.bfloat16)
    pooled = pre_trans.astype(jnp.float32).reshape(
        lot_count, image_count, height // 2, 2, breadth // 2, 2, channels
    )
    pooled = jnp.mean(pooled, axis=(3, 5)).astype(jnp.bfloat16)
    trans_first = activate(matmul_rows(pre_trans, trans_in)).astype(jnp.bfloat16)
    trans_second = activate(group_conv(rims(trans_first), trans_grouped_one, 2)).astype(
        jnp.bfloat16
    )
    trans_third = activate(group_conv(rims(trans_second), trans_grouped_two, 1)).astype(
        jnp.bfloat16
    )
    result = matmul_rows(pooled, trans_short) + RESIDUAL_SCALE * matmul_rows(trans_third, trans_out)
    return result.astype(jnp.bfloat16)


def local(
    images,
    block_in,
    block_grouped_one,
    block_grouped_two,
    block_out,
    trans_in,
    trans_grouped_one,
    trans_grouped_two,
    trans_out,
    trans_short,
):
    pre_block = (activate(images.astype(jnp.float32)) * BETA_BLOCK).astype(jnp.bfloat16)
    first_mid = activate(matmul_rows(pre_block, block_in)).astype(jnp.bfloat16)
    second_mid = activate(group_conv(plane_rims(first_mid), block_grouped_one, 1)).astype(
        jnp.bfloat16
    )
    third_mid = activate(group_conv(plane_rims(second_mid), block_grouped_two, 1)).astype(
        jnp.bfloat16
    )
    block_result = (
        images.astype(jnp.float32) + RESIDUAL_SCALE * matmul_rows(third_mid, block_out)
    ).astype(jnp.bfloat16)
    weights_all = (trans_in, trans_grouped_one, trans_grouped_two, trans_out, trans_short)
    features = transition(relayout(block_result), weights_all, strip_rims)
    return features


def solution(mesh):
    in_specs = (P("section", None, "row", "col", None), P(), P(), P(), P(), P(), P(), P(), P(), P())
    out_specs = P("section", "row", "col", None, None)
    return jax.shard_map(local, mesh=mesh, in_specs=in_specs, out_specs=out_specs, check_vma=False)
```

profile of v0, /device:TPU:24, one launch (start us, length us, event | category | flops | bytes accessed | tf_op | source)
XLA Modules:
  0.0 262.1 jit_solution(8434279550433340408)
XLA Ops:
  10.5 3.8 %collective-permute-start = (bf16[1,8,1,10,256]{4,1,3,2,0:T(8,128)(2,1)S(1)}, bf16[1,8,1,10,256]{4,1,3,2,0:T(8,128)(2,1)S(1)}, u32[]{:S(2)}, u32[]{:S(2)}) collective-permute-start(bf16[1,8,1,10,256]{4,1,3,2,0:T(8,128)(2,1)S(1)} %get-tuple-element.40), channel_id=1, source_target_pairs={{0,8},{8,16},{16,24},{24,32},{32,40},{40,48},{48,56},{1,9},{9,17},... | collective-permute-start | bytes 122888 | tf_op jit(solution)/shard_map/ppermute | solution.py:17
  16.0 4.2 %collective-permute-done.1 = bf16[1,8,1,10,256]{4,1,3,2,0:T(8,128)(2,1)S(1)} collective-permute-done((bf16[1,8,1,10,256]{4,1,3,2,0:T(8,128)(2,1)S(1)}, bf16[1,8,1,10,256]{4,1,3,2,0:T(8,128)(2,1)S(1)}, u32[]{:S(2)}, u32[]{:S(2)}) %collective-permute-start.1) | collective-permute-done | bytes 40992 | tf_op jit(solution)/shard_map/ppermute | solution.py:20
  20.9 4.6 %collective-permute-start.2 = (bf16[1,8,12,1,256]{4,1,3,2,0:T(8,128)(2,1)}, bf16[1,8,12,1,256]{4,1,3,2,0:T(8,128)(2,1)S(1)}, u32[]{:S(2)}, u32[]{:S(2)}) collective-permute-start(bf16[1,8,12,1,256]{4,1,3,2,0:T(8,128)(2,1)} %get-tuple-element.36), channel_id=1, source_target_pairs={{0,1},{1,2},{2,3},{3,4},{4,5},{5,6},{6,7},{8,9},{9,10},{10,11},{11... | collective-permute-start | bytes 147464 | tf_op jit(solution)/shard_map/ppermute | solution.py:17
  28.3 6.9 %collective-permute-done.3 = bf16[1,8,12,1,256]{4,1,3,2,0:T(8,128)(2,1)S(1)} collective-permute-done((bf16[1,8,12,1,256]{4,1,3,2,0:T(8,128)(2,1)}, bf16[1,8,12,1,256]{4,1,3,2,0:T(8,128)(2,1)S(1)}, u32[]{:S(2)}, u32[]{:S(2)}) %collective-permute-start.3) | collective-permute-done | bytes 49184 | tf_op jit(solution)/shard_map/ppermute | solution.py:20
  40.1 3.8 %collective-permute-start.4 = (bf16[1,8,1,10,256]{4,1,3,2,0:T(8,128)(2,1)S(1)}, bf16[1,8,1,10,256]{4,1,3,2,0:T(8,128)(2,1)S(1)}, u32[]{:S(2)}, u32[]{:S(2)}) collective-permute-start(bf16[1,8,1,10,256]{4,1,3,2,0:T(8,128)(2,1)S(1)} %get-tuple-element.38), channel_id=1, source_target_pairs={{0,8},{8,16},{16,24},{24,32},{32,40},{40,48},{48,56},{1,9},{9,17},... | collective-permute-start | bytes 122888 | tf_op jit(solution)/shard_map/ppermute | solution.py:17
  45.6 5.3 %collective-permute-done.5 = bf16[1,8,1,10,256]{4,1,3,2,0:T(8,128)(2,1)S(1)} collective-permute-done((bf16[1,8,1,10,256]{4,1,3,2,0:T(8,128)(2,1)S(1)}, bf16[1,8,1,10,256]{4,1,3,2,0:T(8,128)(2,1)S(1)}, u32[]{:S(2)}, u32[]{:S(2)}) %collective-permute-start.5) | collective-permute-done | bytes 40992 | tf_op jit(solution)/shard_map/ppermute | solution.py:20
  53.4 4.1 %collective-permute-start.7 = (bf16[1,8,12,1,256]{4,1,3,2,0:T(8,128)(2,1)}, bf16[1,8,12,1,256]{4,1,3,2,0:T(8,128)(2,1)S(1)}, u32[]{:S(2)}, u32[]{:S(2)}) collective-permute-start(bf16[1,8,12,1,256]{4,1,3,2,0:T(8,128)(2,1)} %get-tuple-element.35), channel_id=1, source_target_pairs={{1,0},{2,1},{3,2},{4,3},{5,4},{6,5},{7,6},{9,8},{10,9},{11,10},{12... | collective-permute-start | bytes 147464 | tf_op jit(solution)/shard_map/ppermute | solution.py:20
  58.5 4.7 %collective-permute-done.7 = bf16[1,8,12,1,256]{4,1,3,2,0:T(8,128)(2,1)S(1)} collective-permute-done((bf16[1,8,12,1,256]{4,1,3,2,0:T(8,128)(2,1)}, bf16[1,8,12,1,256]{4,1,3,2,0:T(8,128)(2,1)S(1)}, u32[]{:S(2)}, u32[]{:S(2)}) %collective-permute-start.7) | collective-permute-done | bytes 49184 | tf_op jit(solution)/shard_map/ppermute | solution.py:20
  68.5 35.7 %all_to_all.21 = bf16[1,8,10,10,512]{4,3,2,0,1:T(8,128)(2,1)} all-to-all(bf16[1,8,10,10,512]{4,3,2,0,1:T(8,128)(2,1)S(1)} %copy.260), channel_id=1, replica_groups=mesh['section'=4,'row'=8,'col'=8] {'row'}, dimensions={1} | all-to-all | bytes 1638400 | tf_op jit(solution)/shard_map/all_to_all | solution.py:80
  104.2 4.5 %all-to-all-start.1 = ((bf16[1,1,80,10,512]{4,3,1,0,2:T(8,128)(2,1)}), bf16[1,1,80,10,512]{4,3,1,0,2:T(8,128)(2,1)}, u32[]{:S(2)}, u32[]{:S(2)}) async-start(bf16[1,1,80,10,512]{4,3,1,0,2:T(8,128)(2,1)} %bitcast.160), calls=%async_computation.1 | async-start | bytes 2621440 | tf_op jit(solution)/shard_map/all_to_all | solution.py:79
  108.7 4.7 %reshape.597 = bf16[9,128,6,128]{3,2,1,0:T(8,128)(2,1)} reshape(bf16[1152,768]{1,0:T(8,128)(2,1)} %param.16) | data formatting | bytes 3538944 | tf_op jit(solution)/shard_map/reshape | solution.py:64
  113.4 4.7 %reshape.601 = bf16[9,128,6,128]{3,2,1,0:T(8,128)(2,1)} reshape(bf16[1152,768]{1,0:T(8,128)(2,1)} %param.17) | data formatting | bytes 3538944 | tf_op jit(solution)/shard_map/reshape | solution.py:64
  120.6 4.4 %reshape.605 = f32[1,1,8,10,10,512]{5,1,4,3,2,0:T(1,128)} reshape(bf16[1,1,80,10,512]{4,3,1,0,2:T(8,128)(2,1)} %all-to-all-done.1) | data formatting | bytes 2457600 | tf_op jit(solution)/shard_map/convert_element_type | solution.py:91
  125.0 3.4 %copy.268 = f32[1,1,10,8,10,512]{5,4,3,2,1,0:T(8,128)} copy(f32[1,1,10,8,10,512]{5,1,4,2,3,0:T(1,128)} %bitcast.155) | data formatting | bytes 3276800 | tf_op jit(solution)/shard_map/convert_element_type | solution.py:91
  137.3 4.5 %collective-permute-start.8 = (bf16[1,1,1,80,768]{4,3,2,1,0:T(8,128)(2,1)S(1)}, bf16[1,1,1,80,768]{4,3,2,1,0:T(8,128)(2,1)S(1)}, u32[]{:S(2)}, u32[]{:S(2)}) collective-permute-start(bf16[1,1,1,80,768]{4,3,2,1,0:T(8,128)(2,1)S(1)} %get-tuple-element.5), channel_id=1, source_target_pairs={{0,1},{1,2},{2,3},{3,4},{4,5},{5,6},{6,7},{8,9},{9,10},{10,11},{11... | collective-permute-start | bytes 368648 | tf_op jit(solution)/shard_map/ppermute | solution.py:17
  145.5 6.8 %collective-permute-done.9 = bf16[1,1,1,80,768]{4,3,2,1,0:T(8,128)(2,1)S(1)} collective-permute-done((bf16[1,1,1,80,768]{4,3,2,1,0:T(8,128)(2,1)S(1)}, bf16[1,1,1,80,768]{4,3,2,1,0:T(8,128)(2,1)S(1)}, u32[]{:S(2)}, u32[]{:S(2)}) %collective-permute-start.9) | collective-permute-done | bytes 122912 | tf_op jit(solution)/shard_map/ppermute | solution.py:20
  153.9 3.7 %slice.172 = bf16[1,5,40,768]{3,2,1,0:T(8,128)(2,1)} slice(bf16[1,12,82,768]{3,2,1,0:T(8,128)(2,1)} %fusion.51), slice={[0:1:1], [1:10:2], [1:80:2], [0:768:1]} | slice | bytes 614400 | tf_op jit(solution)/shard_map/slice | solution.py:49
  157.6 3.8 %slice.173 = bf16[1,5,40,768]{3,2,1,0:T(8,128)(2,1)} slice(bf16[1,12,82,768]{3,2,1,0:T(8,128)(2,1)} %fusion.51), slice={[0:1:1], [1:10:2], [2:81:2], [0:768:1]} | slice | bytes 614400 | tf_op jit(solution)/shard_map/slice | solution.py:49
  161.4 3.8 %slice.174 = bf16[1,5,40,768]{3,2,1,0:T(8,128)(2,1)} slice(bf16[1,12,82,768]{3,2,1,0:T(8,128)(2,1)} %fusion.51), slice={[0:1:1], [1:10:2], [3:82:2], [0:768:1]} | slice | bytes 614400 | tf_op jit(solution)/shard_map/slice | solution.py:49
  165.2 3.7 %slice.175 = bf16[1,5,40,768]{3,2,1,0:T(8,128)(2,1)} slice(bf16[1,12,82,768]{3,2,1,0:T(8,128)(2,1)} %fusion.51), slice={[0:1:1], [2:11:2], [1:80:2], [0:768:1]} | slice | bytes 614400 | tf_op jit(solution)/shard_map/slice | solution.py:49
  169.0 3.8 %slice.176 = bf16[1,5,40,768]{3,2,1,0:T(8,128)(2,1)} slice(bf16[1,12,82,768]{3,2,1,0:T(8,128)(2,1)} %fusion.51), slice={[0:1:1], [2:11:2], [2:81:2], [0:768:1]} | slice | bytes 614400 | tf_op jit(solution)/shard_map/slice | solution.py:49
  172.8 3.8 %slice.177 = bf16[1,5,40,768]{3,2,1,0:T(8,128)(2,1)} slice(bf16[1,12,82,768]{3,2,1,0:T(8,128)(2,1)} %fusion.51), slice={[0:1:1], [2:11:2], [3:82:2], [0:768:1]} | slice | bytes 614400 | tf_op jit(solution)/shard_map/slice | solution.py:49
  179.6 3.8 %slice.179 = bf16[1,5,40,768]{3,2,1,0:T(8,128)(2,1)} slice(bf16[1,12,82,768]{3,2,1,0:T(8,128)(2,1)} %fusion.51), slice={[0:1:1], [3:12:2], [2:81:2], [0:768:1]} | slice | bytes 614400 | tf_op jit(solution)/shard_map/slice | solution.py:49
  218.7 4.2 %collective-permute-start.11 = (bf16[1,1,1,40,768]{4,3,2,1,0:T(8,128)(2,1)S(1)}, bf16[1,1,1,40,768]{4,3,2,1,0:T(8,128)(2,1)S(1)}, u32[]{:S(2)}, u32[]{:S(2)}) collective-permute-start(bf16[1,1,1,40,768]{4,3,2,1,0:T(8,128)(2,1)S(1)} %get-tuple-element.43), channel_id=1, source_target_pairs={{1,0},{2,1},{3,2},{4,3},{5,4},{6,5},{7,6},{9,8},{10,9},{11,10},{12... | collective-permute-start | bytes 184328 | tf_op jit(solution)/shard_map/ppermute | solution.py:20
  (148 shorter events, 124.9 us)
Async XLA Ops:
  0.0 259.1 %copy-start = (bf16[768,1536]{1,0:T(8,128)(2,1)S(1)}, bf16[768,1536]{1,0:T(8,128)(2,1)}, u32[]{:S(2)}) copy-start(bf16[768,1536]{1,0:T(8,128)(2,1)} %param.18) | copy-start | bytes 7077892
  6.1 21.3 %copy-start.12 = (bf16[1152,256]{1,0:T(8,128)(2,1)S(1)}, bf16[1152,256]{1,0:T(8,128)(2,1)}, u32[]{:S(2)}) copy-start(bf16[1152,256]{1,0:T(8,128)(2,1)} %param.12) | copy-start | bytes 1769476
  10.5 5.5 %collective-permute-start = (bf16[1,8,1,10,256]{4,1,3,2,0:T(8,128)(2,1)S(1)}, bf16[1,8,1,10,256]{4,1,3,2,0:T(8,128)(2,1)S(1)}, u32[]{:S(2)}, u32[]{:S(2)}) collective-permute-start(bf16[1,8,1,10,256]{4,1,3,2,0:T(8,128)(2,1)S(1)} %get-tuple-element.40), channel_id=1, source_target_pairs={{0,8},{8,16},{16,24},{24,32},{32,40},{40,48},{48,56},{1,9},{9,17},... | collective-permute-start | bytes 122888 | tf_op jit(solution)/shard_map/ppermute | solution.py:17
  14.3 5.9 %collective-permute-start.1 = (bf16[1,8,1,10,256]{4,1,3,2,0:T(8,128)(2,1)S(1)}, bf16[1,8,1,10,256]{4,1,3,2,0:T(8,128)(2,1)S(1)}, u32[]{:S(2)}, u32[]{:S(2)}) collective-permute-start(bf16[1,8,1,10,256]{4,1,3,2,0:T(8,128)(2,1)S(1)} %get-tuple-element.41), channel_id=1, source_target_pairs={{8,0},{16,8},{24,16},{32,24},{40,32},{48,40},{56,48},{9,1},{17,9},... | collective-permute-start | bytes 122888 | tf_op jit(solution)/shard_map/ppermute | solution.py:20
  20.9 7.5 %collective-permute-start.2 = (bf16[1,8,12,1,256]{4,1,3,2,0:T(8,128)(2,1)}, bf16[1,8,12,1,256]{4,1,3,2,0:T(8,128)(2,1)S(1)}, u32[]{:S(2)}, u32[]{:S(2)}) collective-permute-start(bf16[1,8,12,1,256]{4,1,3,2,0:T(8,128)(2,1)} %get-tuple-element.36), channel_id=1, source_target_pairs={{0,1},{1,2},{2,3},{3,4},{4,5},{5,6},{6,7},{8,9},{9,10},{10,11},{11... | collective-permute-start | bytes 147464 | tf_op jit(solution)/shard_map/ppermute | solution.py:17
  25.5 9.8 %collective-permute-start.3 = (bf16[1,8,12,1,256]{4,1,3,2,0:T(8,128)(2,1)}, bf16[1,8,12,1,256]{4,1,3,2,0:T(8,128)(2,1)S(1)}, u32[]{:S(2)}, u32[]{:S(2)}) collective-permute-start(bf16[1,8,12,1,256]{4,1,3,2,0:T(8,128)(2,1)} %get-tuple-element.37), channel_id=1, source_target_pairs={{1,0},{2,1},{3,2},{4,3},{5,4},{6,5},{7,6},{9,8},{10,9},{11,10},{12... | collective-permute-start | bytes 147464 | tf_op jit(solution)/shard_map/ppermute | solution.py:20
  39.4 18.1 %copy-start.13 = (bf16[1152,256]{1,0:T(8,128)(2,1)S(1)}, bf16[1152,256]{1,0:T(8,128)(2,1)}, u32[]{:S(2)}) copy-start(bf16[1152,256]{1,0:T(8,128)(2,1)} %param.13) | copy-start | bytes 1769476
  40.1 5.5 %collective-permute-start.4 = (bf16[1,8,1,10,256]{4,1,3,2,0:T(8,128)(2,1)S(1)}, bf16[1,8,1,10,256]{4,1,3,2,0:T(8,128)(2,1)S(1)}, u32[]{:S(2)}, u32[]{:S(2)}) collective-permute-start(bf16[1,8,1,10,256]{4,1,3,2,0:T(8,128)(2,1)S(1)} %get-tuple-element.38), channel_id=1, source_target_pairs={{0,8},{8,16},{16,24},{24,32},{32,40},{40,48},{48,56},{1,9},{9,17},... | collective-permute-start | bytes 122888 | tf_op jit(solution)/shard_map/ppermute | solution.py:17
  43.9 6.9 %collective-permute-start.5 = (bf16[1,8,1,10,256]{4,1,3,2,0:T(8,128)(2,1)S(1)}, bf16[1,8,1,10,256]{4,1,3,2,0:T(8,128)(2,1)S(1)}, u32[]{:S(2)}, u32[]{:S(2)}) collective-permute-start(bf16[1,8,1,10,256]{4,1,3,2,0:T(8,128)(2,1)S(1)} %get-tuple-element.39), channel_id=1, source_target_pairs={{8,0},{16,8},{24,16},{32,24},{40,32},{48,40},{56,48},{9,1},{17,9},... | collective-permute-start | bytes 122888 | tf_op jit(solution)/shard_map/ppermute | solution.py:20
  51.5 7.0 %collective-permute-start.6 = (bf16[1,8,12,1,256]{4,1,3,2,0:T(8,128)(2,1)}, bf16[1,8,12,1,256]{4,1,3,2,0:T(8,128)(2,1)S(1)}, u32[]{:S(2)}, u32[]{:S(2)}) collective-permute-start(bf16[1,8,12,1,256]{4,1,3,2,0:T(8,128)(2,1)} %get-tuple-element.34), channel_id=1, source_target_pairs={{0,1},{1,2},{2,3},{3,4},{4,5},{5,6},{6,7},{8,9},{9,10},{10,11},{11... | collective-permute-start | bytes 147464 | tf_op jit(solution)/shard_map/ppermute | solution.py:17
  53.4 9.8 %collective-permute-start.7 = (bf16[1,8,12,1,256]{4,1,3,2,0:T(8,128)(2,1)}, bf16[1,8,12,1,256]{4,1,3,2,0:T(8,128)(2,1)S(1)}, u32[]{:S(2)}, u32[]{:S(2)}) collective-permute-start(bf16[1,8,12,1,256]{4,1,3,2,0:T(8,128)(2,1)} %get-tuple-element.35), channel_id=1, source_target_pairs={{1,0},{2,1},{3,2},{4,3},{5,4},{6,5},{7,6},{9,8},{10,9},{11,10},{12... | collective-permute-start | bytes 147464 | tf_op jit(solution)/shard_map/ppermute | solution.py:20
  104.2 16.4 %all-to-all-start.1 = ((bf16[1,1,80,10,512]{4,3,1,0,2:T(8,128)(2,1)}), bf16[1,1,80,10,512]{4,3,1,0,2:T(8,128)(2,1)}, u32[]{:S(2)}, u32[]{:S(2)}) async-start(bf16[1,1,80,10,512]{4,3,1,0,2:T(8,128)(2,1)} %bitcast.160), calls=%async_computation.1 | async-start | bytes 2621440 | tf_op jit(solution)/shard_map/all_to_all | solution.py:79
  136.4 7.6 %copy-start.4 = (f32[1,1,10,8,10,512]{5,1,4,3,2,0:T(1,128)S(1)}, f32[1,1,10,8,10,512]{5,1,4,3,2,0:T(1,128)}, u32[]{:S(2)}) copy-start(f32[1,1,10,8,10,512]{5,1,4,3,2,0:T(1,128)} %copy.262) | copy-start | bytes 4915204
  137.3 8.2 %collective-permute-start.8 = (bf16[1,1,1,80,768]{4,3,2,1,0:T(8,128)(2,1)S(1)}, bf16[1,1,1,80,768]{4,3,2,1,0:T(8,128)(2,1)S(1)}, u32[]{:S(2)}, u32[]{:S(2)}) collective-permute-start(bf16[1,1,1,80,768]{4,3,2,1,0:T(8,128)(2,1)S(1)} %get-tuple-element.5), channel_id=1, source_target_pairs={{0,1},{1,2},{2,3},{3,4},{4,5},{5,6},{6,7},{8,9},{9,10},{10,11},{11... | collective-permute-start | bytes 368648 | tf_op jit(solution)/shard_map/ppermute | solution.py:17
  141.9 10.4 %collective-permute-start.9 = (bf16[1,1,1,80,768]{4,3,2,1,0:T(8,128)(2,1)S(1)}, bf16[1,1,1,80,768]{4,3,2,1,0:T(8,128)(2,1)S(1)}, u32[]{:S(2)}, u32[]{:S(2)}) collective-permute-start(bf16[1,1,1,80,768]{4,3,2,1,0:T(8,128)(2,1)S(1)} %get-tuple-element.6), channel_id=1, source_target_pairs={{1,0},{2,1},{3,2},{4,3},{5,4},{6,5},{7,6},{9,8},{10,9},{11,10},{12... | collective-permute-start | bytes 368648 | tf_op jit(solution)/shard_map/ppermute | solution.py:20
  188.5 11.6 %copy-start.9 = (bf16[1,5,40,768]{3,2,1,0:T(8,128)(2,1)S(1)}, bf16[1,5,40,768]{3,2,1,0:T(8,128)(2,1)}, u32[]{:S(2)}) copy-start(bf16[1,5,40,768]{3,2,1,0:T(8,128)(2,1)} %slice.179) | copy-start | bytes 921604
  200.9 7.4 %copy-start.8 = (bf16[1,5,40,1,6,128]{5,4,2,1,3,0:T(8,128)(2,1)S(1)}, bf16[1,5,40,1,6,128]{5,4,2,1,3,0:T(8,128)(2,1)}, u32[]{:S(2)}) copy-start(bf16[1,5,40,1,6,128]{5,4,2,1,3,0:T(8,128)(2,1)} %stack.145) | copy-start | bytes 921604
  200.9 8.2 %copy-start.6 = (bf16[1,5,40,1,6,128]{5,4,2,1,3,0:T(8,128)(2,1)S(1)}, bf16[1,5,40,1,6,128]{5,4,2,1,3,0:T(8,128)(2,1)}, u32[]{:S(2)}) copy-start(bf16[1,5,40,1,6,128]{5,4,2,1,3,0:T(8,128)(2,1)} %stack.146) | copy-start | bytes 921604
  202.8 8.7 %copy-start.3 = (bf16[9,128,6,128]{3,2,1,0:T(8,128)(2,1)S(1)}, bf16[9,128,6,128]{3,2,1,0:T(8,128)(2,1)}, u32[]{:S(2)}) copy-start(bf16[9,128,6,128]{3,2,1,0:T(8,128)(2,1)} %reshape.597) | copy-start | bytes 5308420
  216.8 9.3 %collective-permute-start.10 = (bf16[1,1,1,40,768]{4,3,2,1,0:T(8,128)(2,1)S(1)}, bf16[1,1,1,40,768]{4,3,2,1,0:T(8,128)(2,1)S(1)}, u32[]{:S(2)}, u32[]{:S(2)}) collective-permute-start(bf16[1,1,1,40,768]{4,3,2,1,0:T(8,128)(2,1)S(1)} %get-tuple-element.42), channel_id=1, source_target_pairs={{0,1},{1,2},{2,3},{3,4},{4,5},{5,6},{6,7},{8,9},{9,10},{10,11},{11... | collective-permute-start | bytes 184328 | tf_op jit(solution)/shard_map/ppermute | solution.py:17
  218.7 9.7 %collective-permute-start.11 = (bf16[1,1,1,40,768]{4,3,2,1,0:T(8,128)(2,1)S(1)}, bf16[1,1,1,40,768]{4,3,2,1,0:T(8,128)(2,1)S(1)}, u32[]{:S(2)}, u32[]{:S(2)}) collective-permute-start(bf16[1,1,1,40,768]{4,3,2,1,0:T(8,128)(2,1)S(1)} %get-tuple-element.43), channel_id=1, source_target_pairs={{1,0},{2,1},{3,2},{4,3},{5,4},{6,5},{7,6},{9,8},{10,9},{11,10},{12... | collective-permute-start | bytes 184328 | tf_op jit(solution)/shard_map/ppermute | solution.py:20
  232.1 10.5 %copy-start.10 = (bf16[1,5,40,768]{3,2,1,0:T(8,128)(2,1)S(1)}, bf16[1,5,40,768]{3,2,1,0:T(8,128)(2,1)}, u32[]{:S(2)}) copy-start(bf16[1,5,40,768]{3,2,1,0:T(8,128)(2,1)} %get-tuple-element.27) | copy-start | bytes 921604
  244.5 8.2 %copy-start.5 = (bf16[1,5,40,1,6,128]{5,4,2,1,3,0:T(8,128)(2,1)S(1)}, bf16[1,5,40,1,6,128]{5,4,2,1,3,0:T(8,128)(2,1)}, u32[]{:S(2)}) copy-start(bf16[1,5,40,1,6,128]{5,4,2,1,3,0:T(8,128)(2,1)} %stack.156) | copy-start | bytes 921604
  246.3 8.7 %copy-start.2 = (bf16[9,128,6,128]{3,2,1,0:T(8,128)(2,1)S(1)}, bf16[9,128,6,128]{3,2,1,0:T(8,128)(2,1)}, u32[]{:S(2)}) copy-start(bf16[9,128,6,128]{3,2,1,0:T(8,128)(2,1)} %reshape.601) | copy-start | bytes 5308420
  (8 other events, 23.9 us)
where the time goes:
time: 264 us; the launch traced here: 262 us
  local copies, waits for them, and re-layouts  121 us (46%)
  starting transfers between devices  40.1 us (15%)
  blocking collectives  35.7 us (14%)
  waiting for transfers between devices  33.6 us (13%)
  matrix products  19.9 us (8%)
  other arithmetic  11.4 us (4%)
    all_to_all x1, blocking collectives, relayout(): lax.all_to_all(tensor, 'row', split_axis=1, concat_axis=2, tiled=True)  35.7 us
    slice x10, local copies, waits for them, and re-layouts, group_conv(): lax.slice(merged, (0, start_row, start_col, 0), (batches, start_row + str...  33.9 us
    another operation x24, local copies, waits for them, and re-layouts, group_conv(): stacked = jnp.stack(tap_list, axis=3)  30.4 us
    ppermute x6, waiting for transfers between devices, with_halo(): lax.ppermute(lax.slice_in_dim(block, 0, width, axis=dim), axis, backward)  30.3 us
    unnamed x70, local copies, waits for them, and re-layouts  24.3 us
    ppermute x6, starting transfers between devices, with_halo(): lax.ppermute(lax.slice_in_dim(block, block.shape[dim] - width, None, axis...  20.6 us
    ppermute x6, starting transfers between devices, with_halo(): lax.ppermute(lax.slice_in_dim(block, 0, width, axis=dim), axis, backward)  15 us
    convert_element_type x4, local copies, waits for them, and re-layouts, transition(): block_result.astype(jnp.float32)  13.2 us
  transfers between devices with their start and end apart: 13, of which 9 were waited for; matrix products, arithmetic and copies ran while one was open for 6% of the time, Pallas kernels for 0%

commit v1 on v0

--- a/solution.py
+++ b/solution.py
@@ -76,12 +76,18 @@
 
 
 def relayout(tensor):
-    return lax.all_to_all(
-        lax.all_to_all(tensor, "row", split_axis=1, concat_axis=2, tiled=True),
-        "col",
-        split_axis=2,
-        concat_axis=3,
-        tiled=True,
+
+    def step_on_column(view, comm_axis):
+        finding = jnp.concatenate(
+            lax.all_to_all(
+                jnp.stack(jnp.split(view, lax.axis_size(comm_axis), 2), 0), comm_axis, 0, 0
+            ),
+            3,
+        )
+        return finding
+
+    return step_on_column(
+        lax.all_to_all(tensor, "row", split_axis=1, concat_axis=2, tiled=True), "col"
     )
 
 

time: 264 us -> 266 us (level)
    convert_element_type x4 -> x3, local copies, waits for them, and re-layouts: 13.2 us -> 7.53 us  [transition(): block_result.astype(jnp.float32)]
    unnamed x70 -> x75, local copies, waits for them, and re-layouts: 24.3 us -> 29.3 us
where the time goes in v1:
time: 266 us; the launch traced here: 264 us
  local copies, waits for them, and re-layouts  121 us (45%)
  starting transfers between devices  40.1 us (15%)
  blocking collectives  35.6 us (13%)
  waiting for transfers between devices  33.6 us (13%)
  matrix products  19.9 us (7%)
  other arithmetic  13.1 us (5%)
    all_to_all x1, blocking collectives, relayout(): lax.all_to_all(tensor, 'row', split_axis=1, concat_axis=2, tiled=True)  35.6 us
    slice x10, local copies, waits for them, and re-layouts, group_conv(): lax.slice(merged, (0, start_row, start_col, 0), (batches, start_row + str...  33.9 us
    ppermute x6, waiting for transfers between devices, with_halo(): lax.ppermute(lax.slice_in_dim(block, 0, width, axis=dim), axis, backward)  30.3 us
    another operation x24, local copies, waits for them, and re-layouts, group_conv(): stacked = jnp.stack(tap_list, axis=3)  30.3 us
    unnamed x75, local copies, waits for them, and re-layouts  29.3 us
    ppermute x6, starting transfers between devices, with_halo(): lax.ppermute(lax.slice_in_dim(block, block.shape[dim] - width, None, axis...  20.6 us
    ppermute x6, starting transfers between devices, with_halo(): lax.ppermute(lax.slice_in_dim(block, 0, width, axis=dim), axis, backward)  15 us
    reshape x4, local copies, waits for them, and re-layouts, group_conv(): kernel = weight.reshape(9, group_width, groups, group_width)  11.2 us
  transfers between devices with their start and end apart: 13, of which 9 were waited for; matrix products, arithmetic and copies ran while one was open for 6% of the time, Pallas kernels for 0%

profile of v1, /device:TPU:24, one launch (start us, length us, event | category | flops | bytes accessed | tf_op | source)
XLA Modules:
  0.0 263.6 jit_solution(1081888083087245933)
XLA Ops:
  10.5 3.8 %collective-permute-start = (bf16[1,8,1,10,256]{4,1,3,2,0:T(8,128)(2,1)S(1)}, bf16[1,8,1,10,256]{4,1,3,2,0:T(8,128)(2,1)S(1)}, u32[]{:S(2)}, u32[]{:S(2)}) collective-permute-start(bf16[1,8,1,10,256]{4,1,3,2,0:T(8,128)(2,1)S(1)} %get-tuple-element.40), channel_id=1, source_target_pairs={{0,8},{8,16},{16,24},{24,32},{32,40},{40,48},{48,56},{1,9},{9,17},... | collective-permute-start | bytes 122888 | tf_op jit(solution)/shard_map/ppermute | solution.py:17
  16.0 4.2 %collective-permute-done.1 = bf16[1,8,1,10,256]{4,1,3,2,0:T(8,128)(2,1)S(1)} collective-permute-done((bf16[1,8,1,10,256]{4,1,3,2,0:T(8,128)(2,1)S(1)}, bf16[1,8,1,10,256]{4,1,3,2,0:T(8,128)(2,1)S(1)}, u32[]{:S(2)}, u32[]{:S(2)}) %collective-permute-start.1) | collective-permute-done | bytes 40992 | tf_op jit(solution)/shard_map/ppermute | solution.py:20
  20.8 4.6 %collective-permute-start.2 = (bf16[1,8,12,1,256]{4,1,3,2,0:T(8,128)(2,1)}, bf16[1,8,12,1,256]{4,1,3,2,0:T(8,128)(2,1)S(1)}, u32[]{:S(2)}, u32[]{:S(2)}) collective-permute-start(bf16[1,8,12,1,256]{4,1,3,2,0:T(8,128)(2,1)} %get-tuple-element.36), channel_id=1, source_target_pairs={{0,1},{1,2},{2,3},{3,4},{4,5},{5,6},{6,7},{8,9},{9,10},{10,11},{11... | collective-permute-start | bytes 147464 | tf_op jit(solution)/shard_map/ppermute | solution.py:17
  28.3 6.9 %collective-permute-done.3 = bf16[1,8,12,1,256]{4,1,3,2,0:T(8,128)(2,1)S(1)} collective-permute-done((bf16[1,8,12,1,256]{4,1,3,2,0:T(8,128)(2,1)}, bf16[1,8,12,1,256]{4,1,3,2,0:T(8,128)(2,1)S(1)}, u32[]{:S(2)}, u32[]{:S(2)}) %collective-permute-start.3) | collective-permute-done | bytes 49184 | tf_op jit(solution)/shard_map/ppermute | solution.py:20
  40.0 3.8 %collective-permute-start.4 = (bf16[1,8,1,10,256]{4,1,3,2,0:T(8,128)(2,1)S(1)}, bf16[1,8,1,10,256]{4,1,3,2,0:T(8,128)(2,1)S(1)}, u32[]{:S(2)}, u32[]{:S(2)}) collective-permute-start(bf16[1,8,1,10,256]{4,1,3,2,0:T(8,128)(2,1)S(1)} %get-tuple-element.38), channel_id=1, source_target_pairs={{0,8},{8,16},{16,24},{24,32},{32,40},{40,48},{48,56},{1,9},{9,17},... | collective-permute-start | bytes 122888 | tf_op jit(solution)/shard_map/ppermute | solution.py:17
  45.5 5.3 %collective-permute-done.5 = bf16[1,8,1,10,256]{4,1,3,2,0:T(8,128)(2,1)S(1)} collective-permute-done((bf16[1,8,1,10,256]{4,1,3,2,0:T(8,128)(2,1)S(1)}, bf16[1,8,1,10,256]{4,1,3,2,0:T(8,128)(2,1)S(1)}, u32[]{:S(2)}, u32[]{:S(2)}) %collective-permute-start.5) | collective-permute-done | bytes 40992 | tf_op jit(solution)/shard_map/ppermute | solution.py:20
  53.4 4.1 %collective-permute-start.7 = (bf16[1,8,12,1,256]{4,1,3,2,0:T(8,128)(2,1)}, bf16[1,8,12,1,256]{4,1,3,2,0:T(8,128)(2,1)S(1)}, u32[]{:S(2)}, u32[]{:S(2)}) collective-permute-start(bf16[1,8,12,1,256]{4,1,3,2,0:T(8,128)(2,1)} %get-tuple-element.35), channel_id=1, source_target_pairs={{1,0},{2,1},{3,2},{4,3},{5,4},{6,5},{7,6},{9,8},{10,9},{11,10},{12... | collective-permute-start | bytes 147464 | tf_op jit(solution)/shard_map/ppermute | solution.py:20
  58.4 4.7 %collective-permute-done.7 = bf16[1,8,12,1,256]{4,1,3,2,0:T(8,128)(2,1)S(1)} collective-permute-done((bf16[1,8,12,1,256]{4,1,3,2,0:T(8,128)(2,1)}, bf16[1,8,12,1,256]{4,1,3,2,0:T(8,128)(2,1)S(1)}, u32[]{:S(2)}, u32[]{:S(2)}) %collective-permute-start.7) | collective-permute-done | bytes 49184 | tf_op jit(solution)/shard_map/ppermute | solution.py:20
  68.5 35.6 %all_to_all.17 = bf16[1,8,10,10,512]{4,3,2,0,1:T(8,128)(2,1)S(1)} all-to-all(bf16[1,8,10,10,512]{4,3,2,0,1:T(8,128)(2,1)S(1)} %copy.194), channel_id=1, replica_groups=mesh['section'=4,'row'=8,'col'=8] {'row'}, dimensions={1} | all-to-all | bytes 1638400 | tf_op jit(solution)/shard_map/all_to_all | solution.py:90
  109.5 4.5 %all-to-all-start.1 = ((bf16[8,1,1,10,10,512]{5,4,3,2,1,0:T(8,128)(2,1)}), bf16[8,1,1,10,10,512]{5,4,3,2,1,0:T(8,128)(2,1)}, u32[]{:S(2)}, u32[]{:S(2)}) async-start(bf16[8,1,1,10,10,512]{5,4,3,2,1,0:T(8,128)(2,1)} %fusion.139), calls=%async_computation.1 | async-start | bytes 2621440 | tf_op jit(solution)/shard_map/all_to_all | solution.py:82
  114.1 4.7 %reshape.595 = bf16[9,128,6,128]{3,2,1,0:T(8,128)(2,1)} reshape(bf16[1152,768]{1,0:T(8,128)(2,1)} %param.16) | data formatting | bytes 3538944 | tf_op jit(solution)/shard_map/reshape | solution.py:64
  118.7 4.7 %reshape.599 = bf16[9,128,6,128]{3,2,1,0:T(8,128)(2,1)} reshape(bf16[1152,768]{1,0:T(8,128)(2,1)} %param.17) | data formatting | bytes 3538944 | tf_op jit(solution)/shard_map/reshape | solution.py:64
  138.6 4.5 %collective-permute-start.8 = (bf16[1,1,1,80,768]{4,3,2,1,0:T(8,128)(2,1)S(1)}, bf16[1,1,1,80,768]{4,3,2,1,0:T(8,128)(2,1)S(1)}, u32[]{:S(2)}, u32[]{:S(2)}) collective-permute-start(bf16[1,1,1,80,768]{4,3,2,1,0:T(8,128)(2,1)S(1)} %get-tuple-element.5), channel_id=1, source_target_pairs={{0,1},{1,2},{2,3},{3,4},{4,5},{5,6},{6,7},{8,9},{9,10},{10,11},{11... | collective-permute-start | bytes 368648 | tf_op jit(solution)/shard_map/ppermute | solution.py:17
  146.8 6.8 %collective-permute-done.9 = bf16[1,1,1,80,768]{4,3,2,1,0:T(8,128)(2,1)S(1)} collective-permute-done((bf16[1,1,1,80,768]{4,3,2,1,0:T(8,128)(2,1)S(1)}, bf16[1,1,1,80,768]{4,3,2,1,0:T(8,128)(2,1)S(1)}, u32[]{:S(2)}, u32[]{:S(2)}) %collective-permute-start.9) | collective-permute-done | bytes 122912 | tf_op jit(solution)/shard_map/ppermute | solution.py:20
  155.2 3.7 %slice.172 = bf16[1,5,40,768]{3,2,1,0:T(8,128)(2,1)} slice(bf16[1,12,82,768]{3,2,1,0:T(8,128)(2,1)} %fusion.51), slice={[0:1:1], [1:10:2], [1:80:2], [0:768:1]} | slice | bytes 614400 | tf_op jit(solution)/shard_map/slice | solution.py:49
  158.9 3.8 %slice.173 = bf16[1,5,40,768]{3,2,1,0:T(8,128)(2,1)} slice(bf16[1,12,82,768]{3,2,1,0:T(8,128)(2,1)} %fusion.51), slice={[0:1:1], [1:10:2], [2:81:2], [0:768:1]} | slice | bytes 614400 | tf_op jit(solution)/shard_map/slice | solution.py:49
  162.7 3.8 %slice.174 = bf16[1,5,40,768]{3,2,1,0:T(8,128)(2,1)} slice(bf16[1,12,82,768]{3,2,1,0:T(8,128)(2,1)} %fusion.51), slice={[0:1:1], [1:10:2], [3:82:2], [0:768:1]} | slice | bytes 614400 | tf_op jit(solution)/shard_map/slice | solution.py:49
  166.5 3.8 %slice.175 = bf16[1,5,40,768]{3,2,1,0:T(8,128)(2,1)} slice(bf16[1,12,82,768]{3,2,1,0:T(8,128)(2,1)} %fusion.51), slice={[0:1:1], [2:11:2], [1:80:2], [0:768:1]} | slice | bytes 614400 | tf_op jit(solution)/shard_map/slice | solution.py:49
  170.3 3.8 %slice.176 = bf16[1,5,40,768]{3,2,1,0:T(8,128)(2,1)} slice(bf16[1,12,82,768]{3,2,1,0:T(8,128)(2,1)} %fusion.51), slice={[0:1:1], [2:11:2], [2:81:2], [0:768:1]} | slice | bytes 614400 | tf_op jit(solution)/shard_map/slice | solution.py:49
  174.1 3.8 %slice.177 = bf16[1,5,40,768]{3,2,1,0:T(8,128)(2,1)} slice(bf16[1,12,82,768]{3,2,1,0:T(8,128)(2,1)} %fusion.51), slice={[0:1:1], [2:11:2], [3:82:2], [0:768:1]} | slice | bytes 614400 | tf_op jit(solution)/shard_map/slice | solution.py:49
  180.9 3.8 %slice.179 = bf16[1,5,40,768]{3,2,1,0:T(8,128)(2,1)} slice(bf16[1,12,82,768]{3,2,1,0:T(8,128)(2,1)} %fusion.51), slice={[0:1:1], [3:12:2], [2:81:2], [0:768:1]} | slice | bytes 614400 | tf_op jit(solution)/shard_map/slice | solution.py:49
  184.6 3.1 %slice.180 = bf16[1,5,40,768]{3,2,1,0:T(8,128)(2,1)S(1)} slice(bf16[1,12,82,768]{3,2,1,0:T(8,128)(2,1)} %fusion.51), slice={[0:1:1], [3:12:2], [3:82:2], [0:768:1]} | slice | bytes 614400 | tf_op jit(solution)/shard_map/slice | solution.py:49
  220.0 4.2 %collective-permute-start.11 = (bf16[1,1,1,40,768]{4,3,2,1,0:T(8,128)(2,1)S(1)}, bf16[1,1,1,40,768]{4,3,2,1,0:T(8,128)(2,1)S(1)}, u32[]{:S(2)}, u32[]{:S(2)}) collective-permute-start(bf16[1,1,1,40,768]{4,3,2,1,0:T(8,128)(2,1)S(1)} %get-tuple-element.43), channel_id=1, source_target_pairs={{1,0},{2,1},{3,2},{4,3},{5,4},{6,5},{7,6},{9,8},{10,9},{11,10},{12... | collective-permute-start | bytes 184328 | tf_op jit(solution)/shard_map/ppermute | solution.py:20
  224.3 3.1 %fusion.52 = f32[5,40,1536]{2,1,0:T(8,128)} fusion(bf16[512,1536]{1,0:T(8,128)(2,1)} %param.19, f32[5,40,512]{2,1,0:T(8,128)} %convert_reduce_fusion), kind=kOutput, calls=%fused_computation.65 | convolution fusion | flops 314777600 | bytes 3211264 | tf_op jit(solution)/shard_map/dot_general | solution.py:31
  (154 shorter events, 128.1 us)
Async XLA Ops:
  0.0 260.5 %copy-start = (bf16[768,1536]{1,0:T(8,128)(2,1)S(1)}, bf16[768,1536]{1,0:T(8,128)(2,1)}, u32[]{:S(2)}) copy-start(bf16[768,1536]{1,0:T(8,128)(2,1)} %param.18) | copy-start | bytes 7077892
  6.1 21.3 %copy-start.11 = (bf16[1152,256]{1,0:T(8,128)(2,1)S(1)}, bf16[1152,256]{1,0:T(8,128)(2,1)}, u32[]{:S(2)}) copy-start(bf16[1152,256]{1,0:T(8,128)(2,1)} %param.12) | copy-start | bytes 1769476
  10.5 5.5 %collective-permute-start = (bf16[1,8,1,10,256]{4,1,3,2,0:T(8,128)(2,1)S(1)}, bf16[1,8,1,10,256]{4,1,3,2,0:T(8,128)(2,1)S(1)}, u32[]{:S(2)}, u32[]{:S(2)}) collective-permute-start(bf16[1,8,1,10,256]{4,1,3,2,0:T(8,128)(2,1)S(1)} %get-tuple-element.40), channel_id=1, source_target_pairs={{0,8},{8,16},{16,24},{24,32},{32,40},{40,48},{48,56},{1,9},{9,17},... | collective-permute-start | bytes 122888 | tf_op jit(solution)/shard_map/ppermute | solution.py:17
  14.3 5.9 %collective-permute-start.1 = (bf16[1,8,1,10,256]{4,1,3,2,0:T(8,128)(2,1)S(1)}, bf16[1,8,1,10,256]{4,1,3,2,0:T(8,128)(2,1)S(1)}, u32[]{:S(2)}, u32[]{:S(2)}) collective-permute-start(bf16[1,8,1,10,256]{4,1,3,2,0:T(8,128)(2,1)S(1)} %get-tuple-element.41), channel_id=1, source_target_pairs={{8,0},{16,8},{24,16},{32,24},{40,32},{48,40},{56,48},{9,1},{17,9},... | collective-permute-start | bytes 122888 | tf_op jit(solution)/shard_map/ppermute | solution.py:20
  20.8 7.5 %collective-permute-start.2 = (bf16[1,8,12,1,256]{4,1,3,2,0:T(8,128)(2,1)}, bf16[1,8,12,1,256]{4,1,3,2,0:T(8,128)(2,1)S(1)}, u32[]{:S(2)}, u32[]{:S(2)}) collective-permute-start(bf16[1,8,12,1,256]{4,1,3,2,0:T(8,128)(2,1)} %get-tuple-element.36), channel_id=1, source_target_pairs={{0,1},{1,2},{2,3},{3,4},{4,5},{5,6},{6,7},{8,9},{9,10},{10,11},{11... | collective-permute-start | bytes 147464 | tf_op jit(solution)/shard_map/ppermute | solution.py:17
  25.4 9.8 %collective-permute-start.3 = (bf16[1,8,12,1,256]{4,1,3,2,0:T(8,128)(2,1)}, bf16[1,8,12,1,256]{4,1,3,2,0:T(8,128)(2,1)S(1)}, u32[]{:S(2)}, u32[]{:S(2)}) collective-permute-start(bf16[1,8,12,1,256]{4,1,3,2,0:T(8,128)(2,1)} %get-tuple-element.37), channel_id=1, source_target_pairs={{1,0},{2,1},{3,2},{4,3},{5,4},{6,5},{7,6},{9,8},{10,9},{11,10},{12... | collective-permute-start | bytes 147464 | tf_op jit(solution)/shard_map/ppermute | solution.py:20
  39.4 18.1 %copy-start.12 = (bf16[1152,256]{1,0:T(8,128)(2,1)S(1)}, bf16[1152,256]{1,0:T(8,128)(2,1)}, u32[]{:S(2)}) copy-start(bf16[1152,256]{1,0:T(8,128)(2,1)} %param.13) | copy-start | bytes 1769476
  40.0 5.5 %collective-permute-start.4 = (bf16[1,8,1,10,256]{4,1,3,2,0:T(8,128)(2,1)S(1)}, bf16[1,8,1,10,256]{4,1,3,2,0:T(8,128)(2,1)S(1)}, u32[]{:S(2)}, u32[]{:S(2)}) collective-permute-start(bf16[1,8,1,10,256]{4,1,3,2,0:T(8,128)(2,1)S(1)} %get-tuple-element.38), channel_id=1, source_target_pairs={{0,8},{8,16},{16,24},{24,32},{32,40},{40,48},{48,56},{1,9},{9,17},... | collective-permute-start | bytes 122888 | tf_op jit(solution)/shard_map/ppermute | solution.py:17
  43.9 6.9 %collective-permute-start.5 = (bf16[1,8,1,10,256]{4,1,3,2,0:T(8,128)(2,1)S(1)}, bf16[1,8,1,10,256]{4,1,3,2,0:T(8,128)(2,1)S(1)}, u32[]{:S(2)}, u32[]{:S(2)}) collective-permute-start(bf16[1,8,1,10,256]{4,1,3,2,0:T(8,128)(2,1)S(1)} %get-tuple-element.39), channel_id=1, source_target_pairs={{8,0},{16,8},{24,16},{32,24},{40,32},{48,40},{56,48},{9,1},{17,9},... | collective-permute-start | bytes 122888 | tf_op jit(solution)/shard_map/ppermute | solution.py:20
  51.4 7.0 %collective-permute-start.6 = (bf16[1,8,12,1,256]{4,1,3,2,0:T(8,128)(2,1)}, bf16[1,8,12,1,256]{4,1,3,2,0:T(8,128)(2,1)S(1)}, u32[]{:S(2)}, u32[]{:S(2)}) collective-permute-start(bf16[1,8,12,1,256]{4,1,3,2,0:T(8,128)(2,1)} %get-tuple-element.34), channel_id=1, source_target_pairs={{0,1},{1,2},{2,3},{3,4},{4,5},{5,6},{6,7},{8,9},{9,10},{10,11},{11... | collective-permute-start | bytes 147464 | tf_op jit(solution)/shard_map/ppermute | solution.py:17
  53.4 9.8 %collective-permute-start.7 = (bf16[1,8,12,1,256]{4,1,3,2,0:T(8,128)(2,1)}, bf16[1,8,12,1,256]{4,1,3,2,0:T(8,128)(2,1)S(1)}, u32[]{:S(2)}, u32[]{:S(2)}) collective-permute-start(bf16[1,8,12,1,256]{4,1,3,2,0:T(8,128)(2,1)} %get-tuple-element.35), channel_id=1, source_target_pairs={{1,0},{2,1},{3,2},{4,3},{5,4},{6,5},{7,6},{9,8},{10,9},{11,10},{12... | collective-permute-start | bytes 147464 | tf_op jit(solution)/shard_map/ppermute | solution.py:20
  109.5 16.4 %all-to-all-start.1 = ((bf16[8,1,1,10,10,512]{5,4,3,2,1,0:T(8,128)(2,1)}), bf16[8,1,1,10,10,512]{5,4,3,2,1,0:T(8,128)(2,1)}, u32[]{:S(2)}, u32[]{:S(2)}) async-start(bf16[8,1,1,10,10,512]{5,4,3,2,1,0:T(8,128)(2,1)} %fusion.139), calls=%async_computation.1 | async-start | bytes 2621440 | tf_op jit(solution)/shard_map/all_to_all | solution.py:82
  137.8 7.6 %copy-start.3 = (f32[1,1,10,8,10,512]{5,1,4,3,2,0:T(1,128)S(1)}, f32[1,1,10,8,10,512]{5,1,4,3,2,0:T(1,128)}, u32[]{:S(2)}) copy-start(f32[1,1,10,8,10,512]{5,1,4,3,2,0:T(1,128)} %copy.195) | copy-start | bytes 4915204
  138.6 8.2 %collective-permute-start.8 = (bf16[1,1,1,80,768]{4,3,2,1,0:T(8,128)(2,1)S(1)}, bf16[1,1,1,80,768]{4,3,2,1,0:T(8,128)(2,1)S(1)}, u32[]{:S(2)}, u32[]{:S(2)}) collective-permute-start(bf16[1,1,1,80,768]{4,3,2,1,0:T(8,128)(2,1)S(1)} %get-tuple-element.5), channel_id=1, source_target_pairs={{0,1},{1,2},{2,3},{3,4},{4,5},{5,6},{6,7},{8,9},{9,10},{10,11},{11... | collective-permute-start | bytes 368648 | tf_op jit(solution)/shard_map/ppermute | solution.py:17
  143.2 10.4 %collective-permute-start.9 = (bf16[1,1,1,80,768]{4,3,2,1,0:T(8,128)(2,1)S(1)}, bf16[1,1,1,80,768]{4,3,2,1,0:T(8,128)(2,1)S(1)}, u32[]{:S(2)}, u32[]{:S(2)}) collective-permute-start(bf16[1,1,1,80,768]{4,3,2,1,0:T(8,128)(2,1)S(1)} %get-tuple-element.6), channel_id=1, source_target_pairs={{1,0},{2,1},{3,2},{4,3},{5,4},{6,5},{7,6},{9,8},{10,9},{11,10},{12... | collective-permute-start | bytes 368648 | tf_op jit(solution)/shard_map/ppermute | solution.py:20
  189.8 11.7 %copy-start.8 = (bf16[1,5,40,768]{3,2,1,0:T(8,128)(2,1)S(1)}, bf16[1,5,40,768]{3,2,1,0:T(8,128)(2,1)}, u32[]{:S(2)}) copy-start(bf16[1,5,40,768]{3,2,1,0:T(8,128)(2,1)} %slice.179) | copy-start | bytes 921604
  202.2 8.3 %copy-start.5 = (bf16[1,5,40,1,6,128]{5,4,2,1,3,0:T(8,128)(2,1)S(1)}, bf16[1,5,40,1,6,128]{5,4,2,1,3,0:T(8,128)(2,1)}, u32[]{:S(2)}) copy-start(bf16[1,5,40,1,6,128]{5,4,2,1,3,0:T(8,128)(2,1)} %stack.182) | copy-start | bytes 921604
  204.1 8.7 %copy-start.2 = (bf16[9,128,6,128]{3,2,1,0:T(8,128)(2,1)S(1)}, bf16[9,128,6,128]{3,2,1,0:T(8,128)(2,1)}, u32[]{:S(2)}) copy-start(bf16[9,128,6,128]{3,2,1,0:T(8,128)(2,1)} %reshape.595) | copy-start | bytes 5308420
  218.1 9.2 %collective-permute-start.10 = (bf16[1,1,1,40,768]{4,3,2,1,0:T(8,128)(2,1)S(1)}, bf16[1,1,1,40,768]{4,3,2,1,0:T(8,128)(2,1)S(1)}, u32[]{:S(2)}, u32[]{:S(2)}) collective-permute-start(bf16[1,1,1,40,768]{4,3,2,1,0:T(8,128)(2,1)S(1)} %get-tuple-element.42), channel_id=1, source_target_pairs={{0,1},{1,2},{2,3},{3,4},{4,5},{5,6},{6,7},{8,9},{9,10},{10,11},{11... | collective-permute-start | bytes 184328 | tf_op jit(solution)/shard_map/ppermute | solution.py:17
  220.0 9.7 %collective-permute-start.11 = (bf16[1,1,1,40,768]{4,3,2,1,0:T(8,128)(2,1)S(1)}, bf16[1,1,1,40,768]{4,3,2,1,0:T(8,128)(2,1)S(1)}, u32[]{:S(2)}, u32[]{:S(2)}) collective-permute-start(bf16[1,1,1,40,768]{4,3,2,1,0:T(8,128)(2,1)S(1)} %get-tuple-element.43), channel_id=1, source_target_pairs={{1,0},{2,1},{3,2},{4,3},{5,4},{6,5},{7,6},{9,8},{10,9},{11,10},{12... | collective-permute-start | bytes 184328 | tf_op jit(solution)/shard_map/ppermute | solution.py:20
  233.5 10.5 %copy-start.9 = (bf16[1,5,40,768]{3,2,1,0:T(8,128)(2,1)S(1)}, bf16[1,5,40,768]{3,2,1,0:T(8,128)(2,1)}, u32[]{:S(2)}) copy-start(bf16[1,5,40,768]{3,2,1,0:T(8,128)(2,1)} %get-tuple-element.27) | copy-start | bytes 921604
  245.8 7.5 %copy-start.6 = (bf16[1,5,40,1,6,128]{5,4,2,1,3,0:T(8,128)(2,1)S(1)}, bf16[1,5,40,1,6,128]{5,4,2,1,3,0:T(8,128)(2,1)}, u32[]{:S(2)}) copy-start(bf16[1,5,40,1,6,128]{5,4,2,1,3,0:T(8,128)(2,1)} %stack.191) | copy-start | bytes 921604
  245.8 8.3 %copy-start.4 = (bf16[1,5,40,1,6,128]{5,4,2,1,3,0:T(8,128)(2,1)S(1)}, bf16[1,5,40,1,6,128]{5,4,2,1,3,0:T(8,128)(2,1)}, u32[]{:S(2)}) copy-start(bf16[1,5,40,1,6,128]{5,4,2,1,3,0:T(8,128)(2,1)} %stack.192) | copy-start | bytes 921604
  247.7 8.8 %copy-start.1 = (bf16[9,128,6,128]{3,2,1,0:T(8,128)(2,1)S(1)}, bf16[9,128,6,128]{3,2,1,0:T(8,128)(2,1)}, u32[]{:S(2)}) copy-start(bf16[9,128,6,128]{3,2,1,0:T(8,128)(2,1)} %reshape.599) | copy-start | bytes 5308420
  (7 other events, 18.7 us)
